TPU v7x, 256 devices: a whole 4x4x8 slice. The times are simulated.
256 devices in a mesh: blk: 64 (over y_lo, x, z), states: 4 (over y_hi, core).
Axes of the slice: x: 4, y: 4 (y_hi: 2, y_lo: 2; y = y_hi * 2 + y_lo), z: 8, core: 2. Of those that a mesh axis runs over, the one named last changes fastest.
Arguments:
- start_states: float32 [128, 16, 128, 512], P('blk', None, None, 'states'), may hold values from -6 to 6
- couplings: float32 [16, 128, 128], replicated, may hold values from -0.1875 to 0.1875
- potential: float32 [128, 16, 128], P('blk'), may hold values from -18 to 18
- site_offsets: int32 [128, 6, 16], P('blk'), may hold values from 0 to 15
- coupling_index: int32 [128, 7, 16], P('blk'), may hold values from 0 to 15
- degrees: int32 [512], P('states'), may hold values from 1 to 3, as said below
Outputs:
- orthonormal: float32 [128, 16, 128, 512], P('blk', 'states')
Inputs may be any that keep to these rules, and one draw needn't show every extreme that they name: `degrees`: every degree from 1 to 3 belongs to some state.
All inputs are finite; a program needn't handle non-finite values.
Results may differ from a plain program's by a relative error of at most 0.0003.
Values sent between devices are 32-bit elements; how exact they have to be, the bound alone decides.
A program may use at most 128 MiB of HBM per device.

v0:
```python
import jax
import jax.numpy as jnp
from jax import lax
from jax.sharding import PartitionSpec as P

cut_share = 0.3
exact = lax.Precision.HIGHEST


def padded_2(shard, sides, width):
    for axis, dim in sides:
        devices, length = (lax.axis_size(axis), shard.shape[dim])
        up = [(i, (i + 1) % devices) for i in range(devices)]
        down = [(j, i) for i, j in up]
        last = lax.slice_in_dim(shard, length - width, length, axis=dim)
        first = lax.slice_in_dim(shard, 0, width, axis=dim)
        before = lax.ppermute(last, axis, up)
        after = lax.ppermute(first, axis, down)
        shard = jnp.concatenate([before, shard, after], axis=dim)
    return shard


def copy_for_each(shard, axis):
    copies = jnp.broadcast_to(shard, (lax.axis_size(axis), *shard.shape))
    return lax.all_to_all(copies, axis, split_axis=0, concat_axis=0, tiled=True)


def folded_in_pairs(pieces, combine):
    while len(jax.tree.leaves(pieces)[0]) > 1:
        pieces = jax.vmap(combine)(
            *(jax.tree.map(lambda part: part[side::2], pieces) for side in (0, 1))
        )
    return jax.tree.map(lambda part: part[0], pieces)


def joined_all(shard, axis, combine):
    pieces = jax.tree.map(lambda part: copy_for_each(part, axis), shard)
    return folded_in_pairs(pieces, combine)


def coupling_blocks(couplings, index_rows):
    return jnp.take(couplings, index_rows, axis=0)


def apply_inner(padded, blocks_used, onsite, offset_rows):
    middle = padded[1:-1]
    lower_layers = padded[:-2]
    upper_layers = padded[2:]
    count = onsite.shape[1]
    site_ids = jnp.arange(count, dtype=jnp.int32)
    layer_ids = jnp.arange(middle.shape[0], dtype=jnp.int32)
    pieces = [middle]
    for slot in range(1, 7):
        if slot == 5:
            source = lower_layers
        elif slot == 6:
            source = upper_layers
        else:
            source = middle
        neighbour = (site_ids[None, :] + offset_rows[:, slot - 1, :]) % count
        pieces.append(source[layer_ids[:, None], neighbour])
    stacked = jnp.stack(pieces, axis=1)
    summed = jnp.einsum("lksij,lksjn->lsin", blocks_used, stacked, precision=exact)
    return summed + onsite[..., None] * middle


def extrema_of(couplings, onsite, index_rows):
    row_abs = jnp.sum(jnp.abs(couplings), axis=2)
    diag_all = jnp.diagonal(couplings, axis1=1, axis2=2)
    table_ids = jnp.arange(couplings.shape[0], dtype=jnp.int32)
    onehot = (index_rows[..., None] == table_ids).astype(jnp.float32)
    picked_abs = jnp.einsum("lksc,ci->lksi", onehot, row_abs, precision=exact)
    picked_diag = jnp.einsum("lsc,ci->lsi", onehot[:, 0], diag_all, precision=exact)
    centers = picked_diag + onsite
    radii = picked_abs[:, 0] - jnp.abs(picked_diag) + jnp.sum(picked_abs[:, 1:], axis=1)
    return (jnp.max(centers + radii), jnp.min(centers - radii))


def combine(first, second):
    return (jnp.maximum(first[0], second[0]), jnp.minimum(first[1], second[1]))


def faces(field):
    return padded_2(field, (("blk", 0),), 1)


def per_device(start_states, couplings, potential, site_offsets, coupling_index, degrees):
    upper, lower = joined_all(extrema_of(couplings, potential, coupling_index), "blk", combine)
    cut_edge = lower + cut_share * (upper - lower)
    middle_value = (upper + cut_edge) / 2.0
    half_width = (upper - cut_edge) / 2.0

    def scaled(applied, field):
        return (applied - middle_value * field) / half_width

    local_blocks = coupling_blocks(couplings, coupling_index)
    first_step = scaled(
        apply_inner(faces(start_states), local_blocks, potential, site_offsets), start_states
    )
    second = (
        2.0
        * scaled(apply_inner(faces(first_step), local_blocks, potential, site_offsets), first_step)
        - start_states
    )
    third = (
        2.0 * scaled(apply_inner(faces(second), local_blocks, potential, site_offsets), second)
        - first_step
    )
    chosen = jnp.where(degrees == 1, first_step, jnp.where(degrees == 2, second, third))
    regrouped = lax.all_to_all(chosen, "states", split_axis=1, concat_axis=3, tiled=True)
    rows = regrouped.reshape(-1, regrouped.shape[-1])
    partial_gram = lax.dot_general(
        rows, rows, (((0,), (0,)), ((), ())), precision=exact, preferred_element_type=jnp.float32
    )
    gram = lax.psum(partial_gram, ("blk", "states"))
    factor = jnp.linalg.cholesky(gram)
    identity = jnp.eye(gram.shape[0], dtype=jnp.float32)
    inverse_factor = jax.scipy.linalg.solve_triangular(factor, identity, lower=True)
    orthonormal = jnp.dot(
        rows, inverse_factor.T, precision=exact, preferred_element_type=jnp.float32
    )
    return orthonormal.reshape(regrouped.shape)


def solution(mesh):
    in_specs = (
        P("blk", None, None, "states"),
        P(),
        P("blk", None, None),
        P("blk", None, None),
        P("blk", None, None),
        P("states"),
    )
    out_specs = P("blk", "states", None, None)
    return jax.shard_map(
        per_device, mesh=mesh, in_specs=in_specs, out_specs=out_specs, check_vma=False
    )
```

profile of v0, /device:TPU:2, one launch (start us, length us, event | category | flops | bytes accessed | tf_op | source)
XLA Modules:
  0.0 722.4 jit_solution(9385407167922655574)
XLA Ops:
  8.1 6.1 copy.46
  18.6 13.0 %all-to-all-start = ((f32[64,1,1]{2,1,0:T(1,128)}), f32[64,1,1]{2,1,0:T(1,128)S(1)}, u32[]{:S(2)}, u32[]{:S(2)}) async-start(f32[64,1,1]{2,1,0:T(1,128)} %broadcast_in_dim.49), calls=%async_computation | async-start | bytes 65536 | tf_op jit(solution)/shard_map/all_to_all | solution.py:25
  55.6 6.7 gather_fusion
  63.7 12.0 %all-to-all-start.1 = ((f32[64,1,1]{2,1,0:T(1,128)}), f32[64,1,1]{2,1,0:T(1,128)S(1)}, u32[]{:S(2)}, u32[]{:S(2)}) async-start(f32[64,1,1]{2,1,0:T(1,128)} %broadcast_in_dim.50), calls=%async_computation.1 | async-start | bytes 65536 | tf_op jit(solution)/shard_map/all_to_all | solution.py:25
  77.5 7.6 %all-to-all-done.1 = f32[64,1,1]{2,1,0:T(1,128)S(1)} async-done(((f32[64,1,1]{2,1,0:T(1,128)}), f32[64,1,1]{2,1,0:T(1,128)S(1)}, u32[]{:S(2)}, u32[]{:S(2)}) %all-to-all-start.1) | async-done | bytes 288 | tf_op jit(solution)/shard_map/all_to_all | solution.py:25
  90.6 4.1 pad_maximum_fusion.4
  108.1 21.0 %bitcast_dynamic-update-slice_fusion.2 = (f32[2,7,16,128,128]{4,3,2,0,1:T(8,128)}, f32[2,16,128,128]{3,2,1,0:T(8,128)S(1)}) fusion(f32[]{:T(128)S(6)} %div.29, f32[2,16,128,128]{3,2,1,0:T(8,128)S(1)} %copy-done.1, f32[]{:T(128)S(6)} %div.28, f32[2,16,128]{2,1,0:T(8,128)S(1)} %copy-done.22, f32[2,7,16,128,128]{4,3,1,2,0:T(8,128)} %constant_dynamic-update-slice_fusion, ...), kind=kOutput, calls=%fused_computation.56 | convolution fusion | flops 5643436032 | bytes 35668200 | tf_op jit(solution)/shard_map/lksij,lksjn->lsin/dot_general | solution.py:63
  173.9 21.6 %bitcast_dynamic-update-slice_fusion.1 = (f32[2,7,16,128,128]{4,3,2,0,1:T(8,128)}, f32[2,16,128,128]{3,2,1,0:T(8,128)}) fusion(f32[2,16,128,128]{3,2,1,0:T(8,128)S(1)} %copy-done.1, f32[]{:T(128)S(6)} %div.29, f32[2,16,128,128]{3,2,1,0:T(8,128)} %copy-done.2, f32[]{:T(128)S(6)} %div.28, f32[2,16,128]{2,1,0:T(8,128)S(1)} %copy-done.22, ...), kind=kOutput, calls=%fused_computation.50 | convolution fusion | flops 5644484608 | bytes 37765352 | tf_op jit(solution)/shard_map/lksij,lksjn->lsin/dot_general | solution.py:63
  221.8 4.3 collective-permute-done.4
  226.0 4.0 pad_maximum_fusion
  241.2 21.2 %fusion.19 = f32[2,16,128,128]{3,2,1,0:T(8,128)} fusion(f32[2,16,128,128]{3,2,1,0:T(8,128)S(1)} %copy-done.4, f32[2,16,128,128]{3,2,1,0:T(8,128)S(1)} %copy-done.6, f32[2,7,16,128,128]{4,3,2,0,1:T(8,128)} %constant_dynamic-update-slice_fusion.12, f32[2,7,16,128,128]{4,3,2,1,0:T(8,128)} %bitcast.190, pred[2,7,16]{1,2,0:T(8,128)(4,1)S(1)} %copy.43, ...), kind=kOutput, calls=%fused_computation.49 | convolution fusion | flops 5645533184 | bytes 35668456 | tf_op jit(solution)/shard_map/lksij,lksjn->lsin/dot_general | solution.py:63
  264.2 31.1 %all_to_all.33 = f32[2,16,128,128]{3,2,0,1:T(8,128)S(1)} all-to-all(f32[2,16,128,128]{3,2,0,1:T(8,128)S(1)} %copy.52), channel_id=1, replica_groups=mesh['blk'=64,'states'=4] {'states'}, dimensions={1} | all-to-all | bytes 4194304 | tf_op jit(solution)/shard_map/all_to_all | solution.py:110
  296.7 4.5 fusion.11
  305.6 250.9 %all-reduce.3.cloned.1.call-done = f32[512,512]{0,1:T(8,128)} async-done(((f32[512,512]{0,1:T(8,128)}), f32[512,512]{0,1:T(8,128)}) %all-reduce.3.cloned.1.call-update) | async-done | bytes 1048592 | tf_op jit(solution)/shard_map/psum | solution.py:115
  561.6 11.7 %cholesky.104 = f32[128,128]{1,0:T(8,128)S(1)} custom-call(f32[128,128]{1,0:T(8,128)S(1)} %cholesky.266), custom_call_target="Cholesky" | custom-call | tf_op jit(solution)/shard_map/jit(cholesky)/cholesky | solution.py:116
  573.5 9.8 %custom-call.31 = f32[1,128,128]{1,2,0:T(8,128)S(1)} custom-call(f32[1,128,128]{2,1,0:T(8,128)S(1)} %get-tuple-element.48), custom_call_target="InvertDiagBlocksLowerTriangular" | custom-call | tf_op jit(solution)/shard_map/jit(cholesky)/cholesky | solution.py:116
  585.8 11.7 %cholesky.217 = f32[128,128]{1,0:T(8,128)S(1)} custom-call(f32[128,128]{1,0:T(8,128)S(1)} %cholesky.270), custom_call_target="Cholesky" | custom-call | tf_op jit(solution)/shard_map/jit(cholesky)/cholesky | solution.py:116
  597.5 10.0 %custom-call.32 = f32[1,128,128]{1,2,0:T(8,128)S(1)} custom-call(f32[1,128,128]{2,1,0:T(8,128)S(1)} %get-tuple-element.45), custom_call_target="InvertDiagBlocksLowerTriangular" | custom-call | tf_op jit(solution)/shard_map/jit(cholesky)/cholesky | solution.py:116
  609.1 11.7 %cholesky.238 = f32[128,128]{1,0:T(8,128)S(1)} custom-call(f32[128,128]{1,0:T(8,128)S(1)} %cholesky.275), custom_call_target="Cholesky" | custom-call | tf_op jit(solution)/shard_map/jit(cholesky)/cholesky | solution.py:116
  620.8 9.8 %custom-call.33 = f32[1,128,128]{1,2,0:T(8,128)S(1)} custom-call(f32[1,128,128]{2,1,0:T(8,128)S(1)} %get-tuple-element.42), custom_call_target="InvertDiagBlocksLowerTriangular" | custom-call | tf_op jit(solution)/shard_map/jit(cholesky)/cholesky | solution.py:116
  632.1 11.7 %cholesky.255 = f32[128,128]{1,0:T(8,128)S(1)} custom-call(f32[128,128]{1,0:T(8,128)S(1)} %convolution_subtract_fusion.5), custom_call_target="Cholesky" | custom-call | tf_op jit(solution)/shard_map/jit(cholesky)/cholesky | solution.py:116
  649.7 13.9 %while.1 = (s32[]{:T(128)}, f32[512,512]{1,0:T(8,128)}, s32[4,2]{0,1:T(2,128)S(1)}, f32[4,128,128]{2,1,0:T(8,128)}, s32[]{:T(128)}) while((s32[]{:T(128)}, f32[512,512]{1,0:T(8,128)}, s32[4,2]{0,1:T(2,128)S(1)}, f32[4,128,128]{2,1,0:T(8,128)}, s32[]{:T(128)}) %tuple.46), condition=%wide.while_cond, body=%wide.while_body.sunk | while | flops 2 | bytes 132205 | solution.py:118
  663.7 40.1 %custom-call.34 = f32[4,128,128]{1,2,0:T(8,128)S(1)} custom-call(f32[4,128,128]{2,1,0:T(8,128)} %get-tuple-element.12), custom_call_target="InvertDiagBlocksLowerTriangular" | custom-call | tf_op jit(solution)/shard_map/jit(_solve_triangular)/triangular_solve | solution.py:118
  710.5 4.8 fusion.30
  (211 shorter events, 173.6 us)
Async XLA Ops:
  8.1 6.2 copy-start.23
  8.1 8.3 %copy-start.22 = (f32[2,16,128]{2,1,0:T(8,128)S(1)}, f32[2,16,128]{2,1,0:T(8,128)}, u32[]{:S(2)}) copy-start(f32[2,16,128]{2,1,0:T(8,128)} %param.8) | copy-start | bytes 49156
  8.1 23.5 %copy-start.1 = (f32[2,16,128,128]{3,2,1,0:T(8,128)S(1)}, f32[2,16,128,128]{3,2,1,0:T(8,128)}, u32[]{:S(2)}) copy-start(f32[2,16,128,128]{3,2,1,0:T(8,128)} %param.6) | copy-start | bytes 6291460
  18.6 43.8 %all-to-all-start = ((f32[64,1,1]{2,1,0:T(1,128)}), f32[64,1,1]{2,1,0:T(1,128)S(1)}, u32[]{:S(2)}, u32[]{:S(2)}) async-start(f32[64,1,1]{2,1,0:T(1,128)} %broadcast_in_dim.49), calls=%async_computation | async-start | bytes 65536 | tf_op jit(solution)/shard_map/all_to_all | solution.py:25
  33.2 57.4 %collective-permute-start.1 = (f32[1,16,128,128]{3,2,1,0:T(8,128)}, f32[1,16,128,128]{3,2,1,0:T(8,128)}, u32[]{:S(2)}, u32[]{:S(2)}) collective-permute-start(f32[1,16,128,128]{3,2,1,0:T(8,128)} %get-tuple-element.37), channel_id=1, source_target_pairs={{4,0},{8,4},{12,8},{16,12},{20,16},{24,20},{28,24},{32,28},{36,32}... | collective-permute-start | bytes 3145736 | tf_op jit(solution)/shard_map/ppermute | solution.py:18
  35.9 54.7 %collective-permute-start = (f32[1,16,128,128]{3,2,1,0:T(8,128)}, f32[1,16,128,128]{3,2,1,0:T(8,128)}, u32[]{:S(2)}, u32[]{:S(2)}) collective-permute-start(f32[1,16,128,128]{3,2,1,0:T(8,128)} %get-tuple-element.38), channel_id=1, source_target_pairs={{0,4},{4,8},{8,12},{12,16},{16,20},{20,24},{24,28},{28,32},{32,36}... | collective-permute-start | bytes 3145736 | tf_op jit(solution)/shard_map/ppermute | solution.py:17
  45.9 3.4 copy-start.8
  49.3 2.3 copy-start.9
  63.7 21.4 %all-to-all-start.1 = ((f32[64,1,1]{2,1,0:T(1,128)}), f32[64,1,1]{2,1,0:T(1,128)S(1)}, u32[]{:S(2)}, u32[]{:S(2)}) async-start(f32[64,1,1]{2,1,0:T(1,128)} %broadcast_in_dim.50), calls=%async_computation.1 | async-start | bytes 65536 | tf_op jit(solution)/shard_map/all_to_all | solution.py:25
  75.6 480.9 %all-reduce.3.cloned.1.call-start = ((), (), s32[]{:S(2)}) async-start(), calls=%async_computation.3 | async-start | bytes 2097152 | tf_op jit(solution)/shard_map/psum | solution.py:115
  131.2 26.2 %collective-permute-start.3 = (f32[1,16,128,128]{3,2,1,0:T(8,128)}, f32[1,16,128,128]{3,2,1,0:T(8,128)S(1)}, u32[]{:S(2)}, u32[]{:S(2)}) collective-permute-start(f32[1,16,128,128]{3,2,1,0:T(8,128)} %get-tuple-element.33), channel_id=1, source_target_pairs={{4,0},{8,4},{12,8},{16,12},{20,16},{24,20},{28,24},{32,28},{36,32}... | collective-permute-start | bytes 3145736 | tf_op jit(solution)/shard_map/ppermute | solution.py:18
  132.9 24.9 %collective-permute-start.2 = (f32[1,16,128,128]{3,2,1,0:T(8,128)}, f32[1,16,128,128]{3,2,1,0:T(8,128)}, u32[]{:S(2)}, u32[]{:S(2)}) collective-permute-start(f32[1,16,128,128]{3,2,1,0:T(8,128)} %get-tuple-element.34), channel_id=1, source_target_pairs={{0,4},{4,8},{8,12},{12,16},{16,20},{20,24},{24,28},{28,32},{32,36}... | collective-permute-start | bytes 3145736 | tf_op jit(solution)/shard_map/ppermute | solution.py:17
  148.0 3.3 copy-start.16
  169.0 3.3 copy-start.18
  195.5 6.8 copy-start.25
  195.5 6.8 copy-start.5
  198.4 23.4 %collective-permute-start.5 = (f32[1,16,128,128]{3,2,1,0:T(8,128)}, f32[1,16,128,128]{3,2,1,0:T(8,128)}, u32[]{:S(2)}, u32[]{:S(2)}) collective-permute-start(f32[1,16,128,128]{3,2,1,0:T(8,128)} %get-tuple-element.29), channel_id=1, source_target_pairs={{4,0},{8,4},{12,8},{16,12},{20,16},{24,20},{28,24},{32,28},{36,32}... | collective-permute-start | bytes 3145736 | tf_op jit(solution)/shard_map/ppermute | solution.py:18
  202.2 23.9 %collective-permute-start.4 = (f32[1,16,128,128]{3,2,1,0:T(8,128)S(1)}, f32[1,16,128,128]{3,2,1,0:T(8,128)}, u32[]{:S(2)}, u32[]{:S(2)}) collective-permute-start(f32[1,16,128,128]{3,2,1,0:T(8,128)S(1)} %get-tuple-element.30), channel_id=1, source_target_pairs={{0,4},{4,8},{8,12},{12,16},{16,20},{20,24},{24,28},{28,32},{32,36}... | collective-permute-start | bytes 3145736 | tf_op jit(solution)/shard_map/ppermute | solution.py:17
  210.5 3.3 copy-start.14
  213.8 2.3 copy-start.13
  238.2 3.0 copy-start.6
  296.7 4.5 copy-start.7
  556.5 2.6 copy-start.19
  649.7 57.0 %copy-start.20 = (f32[512,512]{1,0:T(8,128)S(1)}, f32[512,512]{1,0:T(8,128)}, u32[]{:S(2)}) copy-start(f32[512,512]{1,0:T(8,128)} %fusion.46) | copy-start | bytes 3145732
  (11 other events, 22.6 us)
Sparse Core Ops, SparseCore 0:
  301.3 255.1 all-reduce.2
where the time goes:
time: 730 us; the launch traced here: 722 us
  waiting for transfers between devices  265 us (36%)
  local copies, waits for them, and re-layouts  148 us (20%)
  other arithmetic  138 us (19%)
  matrix products  86.3 us (12%)
  starting transfers between devices  34.2 us (5%)
  blocking collectives  31.1 us (4%)
  between operations  19.3 us (3%)
    psum x1, waiting for transfers between devices, per_device(): gram = lax.psum(partial_gram, ('blk', 'states'))  251 us
    another operation x14, other arithmetic, per_device(): factor = jnp.linalg.cholesky(gram)  78.6 us
    dot_general x3, matrix products, apply_inner(): jnp.einsum('lksij,lksjn->lsin', blocks_used, stacked, precision=exact)  63.8 us
    gather x18, local copies, waits for them, and re-layouts, apply_inner(): pieces.append(source[layer_ids[:, None], neighbour])  50.7 us
    unnamed x69, local copies, waits for them, and re-layouts  48.1 us
    another operation x3, other arithmetic, per_device(): jax.scipy.linalg.solve_triangular(factor, identity, lower=True)  41.4 us
    all_to_all x1, blocking collectives, per_device(): lax.all_to_all(chosen, 'states', split_axis=1, concat_axis=3, tiled=True)  31.1 us
    all_to_all x2, starting transfers between devices, copy_for_each(): return lax.all_to_all(copies, axis, split_axis=0, concat_axis=0, tiled=True)  25 us
  transfers between devices with their start and end apart: 9, of which 5 were waited for; matrix products, arithmetic and copies ran while one was open for 10% of the time, Pallas kernels for 0%

commit v1 on v0

--- a/solution.py
+++ b/solution.py
@@ -112,7 +112,7 @@
     partial_gram = lax.dot_general(
         rows, rows, (((0,), (0,)), ((), ())), precision=exact, preferred_element_type=jnp.float32
     )
-    gram = lax.psum(partial_gram, ("blk", "states"))
+    gram = lax.psum(lax.psum(partial_gram, "states"), "blk")
     factor = jnp.linalg.cholesky(gram)
     identity = jnp.eye(gram.shape[0], dtype=jnp.float32)
     inverse_factor = jax.scipy.linalg.solve_triangular(factor, identity, lower=True)

time: 730 us -> 1140 us (1.56); the launches traced: 722 us -> 1120 us
  waiting for transfers between devices: 265 us -> 660 us
    psum x1 -> x2, waiting for transfers between devices: 251 us -> 646 us  [per_device(): gram = lax.psum(lax.psum(partial_gram, 'states'), 'blk')]
    unnamed x69 -> x65, local copies, waits for them, and re-layouts: 48.1 us -> 48.4 us
  transfers between devices with their start and end apart: 9 -> 10, of which waited for: 5 -> 6; matrix products, arithmetic and copies ran while one was open for 10% -> 7% of each run, Pallas kernels for 0% -> 0%
where the time goes in v1:
time: 1140 us; the launch traced here: 1120 us
  waiting for transfers between devices  660 us (58%)
  local copies, waits for them, and re-layouts  151 us (13%)
  other arithmetic  138 us (12%)
  matrix products  86.8 us (8%)
  starting transfers between devices  34.3 us (3%)
  blocking collectives  31.1 us (3%)
  between operations  19.1 us (2%)
    psum x2, waiting for transfers between devices, per_device(): gram = lax.psum(lax.psum(partial_gram, 'states'), 'blk')  646 us
    another operation x14, other arithmetic, per_device(): factor = jnp.linalg.cholesky(gram)  78.6 us
    dot_general x3, matrix products, apply_inner(): jnp.einsum('lksij,lksjn->lsin', blocks_used, stacked, precision=exact)  64.3 us
    gather x18, local copies, waits for them, and re-layouts, apply_inner(): pieces.append(source[layer_ids[:, None], neighbour])  52 us
    unnamed x65, local copies, waits for them, and re-layouts  48.4 us
    another operation x3, other arithmetic, per_device(): jax.scipy.linalg.solve_triangular(factor, identity, lower=True)  41.4 us
    all_to_all x1, blocking collectives, per_device(): lax.all_to_all(chosen, 'states', split_axis=1, concat_axis=3, tiled=True)  31.1 us
    all_to_all x2, starting transfers between devices, copy_for_each(): return lax.all_to_all(copies, axis, split_axis=0, concat_axis=0, tiled=True)  25 us
  transfers between devices with their start and end apart: 10, of which 6 were waited for; matrix products, arithmetic and copies ran while one was open for 7% of the time, Pallas kernels for 0%

profile of v1, /device:TPU:2, one launch (start us, length us, event | category | flops | bytes accessed | tf_op | source)
XLA Modules:
  0.0 1120.6 jit_solution(2403717683977411480)
XLA Ops:
  8.1 6.1 copy.46
  18.6 13.0 %all-to-all-start = ((f32[64,1,1]{2,1,0:T(1,128)}), f32[64,1,1]{2,1,0:T(1,128)S(1)}, u32[]{:S(2)}, u32[]{:S(2)}) async-start(f32[64,1,1]{2,1,0:T(1,128)} %broadcast_in_dim.49), calls=%async_computation | async-start | bytes 65536 | tf_op jit(solution)/shard_map/all_to_all | solution.py:25
  55.5 6.7 gather_fusion
  63.5 12.0 %all-to-all-start.1 = ((f32[64,1,1]{2,1,0:T(1,128)}), f32[64,1,1]{2,1,0:T(1,128)S(1)}, u32[]{:S(2)}, u32[]{:S(2)}) async-start(f32[64,1,1]{2,1,0:T(1,128)} %broadcast_in_dim.50), calls=%async_computation.1 | async-start | bytes 65536 | tf_op jit(solution)/shard_map/all_to_all | solution.py:25
  77.4 7.6 all-to-all-done.1
  107.7 21.4 %bitcast_dynamic-update-slice_fusion.2 = (f32[2,7,16,128,128]{4,3,2,0,1:T(8,128)}, f32[2,16,128,128]{3,2,1,0:T(8,128)}) fusion(f32[]{:T(128)S(6)} %div.29, f32[2,16,128,128]{3,2,1,0:T(8,128)S(1)} %copy-done.1, f32[]{:T(128)S(6)} %div.28, f32[2,16,128]{2,1,0:T(8,128)S(1)} %copy-done.20, f32[2,7,16,128,128]{4,3,1,2,0:T(8,128)} %constant_dynamic-update-slice_fusion, ...), kind=kOutput, calls=%fused_computation.56 | convolution fusion | flops 5643436032 | bytes 35668200 | tf_op jit(solution)/shard_map/lksij,lksjn->lsin/dot_general | solution.py:63
  158.9 4.0 pad_maximum_fusion.2
  175.0 21.6 %bitcast_dynamic-update-slice_fusion.1 = (f32[2,7,16,128,128]{4,3,2,0,1:T(8,128)}, f32[2,16,128,128]{3,2,1,0:T(8,128)}) fusion(f32[2,16,128,128]{3,2,1,0:T(8,128)S(1)} %copy-done.1, f32[]{:T(128)S(6)} %div.29, f32[2,16,128,128]{3,2,1,0:T(8,128)} %get-tuple-element.62, f32[]{:T(128)S(6)} %div.28, f32[2,16,128]{2,1,0:T(8,128)S(1)} %copy-done.20, ...), kind=kOutput, calls=%fused_computation.50 | convolution fusion | flops 5644484608 | bytes 37765352 | tf_op jit(solution)/shard_map/lksij,lksjn->lsin/dot_general | solution.py:63
  223.3 4.5 collective-permute-done.4
  244.6 21.2 %fusion.19 = f32[2,16,128,128]{3,2,1,0:T(8,128)} fusion(f32[2,16,128,128]{3,2,1,0:T(8,128)S(1)} %copy-done.3, f32[2,16,128,128]{3,2,1,0:T(8,128)S(1)} %copy-done.4, f32[2,7,16,128,128]{4,3,2,0,1:T(8,128)} %constant_dynamic-update-slice_fusion.12, f32[2,7,16,128,128]{4,3,2,1,0:T(8,128)} %bitcast.190, pred[2,7,16]{1,2,0:T(8,128)(4,1)S(1)} %copy.43, ...), kind=kOutput, calls=%fused_computation.49 | convolution fusion | flops 5645533184 | bytes 35668456 | tf_op jit(solution)/shard_map/lksij,lksjn->lsin/dot_general | solution.py:63
  267.5 31.1 %all_to_all.33 = f32[2,16,128,128]{3,2,0,1:T(8,128)S(1)} all-to-all(f32[2,16,128,128]{3,2,0,1:T(8,128)S(1)} %copy.52), channel_id=1, replica_groups=mesh['blk'=64,'states'=4] {'states'}, dimensions={1} | all-to-all | bytes 4194304 | tf_op jit(solution)/shard_map/all_to_all | solution.py:110
  300.0 4.5 fusion.11
  304.6 46.5 %all-reduce.4.cloned.1.call-done = f32[512,512]{0,1:T(8,128)} async-done(((f32[512,512]{0,1:T(8,128)}), f32[512,512]{0,1:T(8,128)}) %all-reduce.4.cloned.1.call-update) | async-done | bytes 1048592 | tf_op jit(solution)/shard_map/psum | solution.py:115
  355.6 599.0 %all-reduce.6.cloned.1.call-done = f32[512,512]{0,1:T(8,128)} async-done(((f32[512,512]{0,1:T(8,128)}), f32[512,512]{0,1:T(8,128)}) %all-reduce.6.cloned.1.call-update) | async-done | bytes 1048592 | tf_op jit(solution)/shard_map/psum | solution.py:115
  959.7 11.7 %cholesky.104 = f32[128,128]{1,0:T(8,128)S(1)} custom-call(f32[128,128]{1,0:T(8,128)S(1)} %cholesky.266), custom_call_target="Cholesky" | custom-call | tf_op jit(solution)/shard_map/jit(cholesky)/cholesky | solution.py:116
  971.6 9.8 custom-call.31
  983.9 11.7 %cholesky.217 = f32[128,128]{1,0:T(8,128)S(1)} custom-call(f32[128,128]{1,0:T(8,128)S(1)} %cholesky.270), custom_call_target="Cholesky" | custom-call | tf_op jit(solution)/shard_map/jit(cholesky)/cholesky | solution.py:116
  995.6 10.0 custom-call.32
  1007.2 11.7 %cholesky.238 = f32[128,128]{1,0:T(8,128)S(1)} custom-call(f32[128,128]{1,0:T(8,128)S(1)} %cholesky.275), custom_call_target="Cholesky" | custom-call | tf_op jit(solution)/shard_map/jit(cholesky)/cholesky | solution.py:116
  1018.9 9.8 custom-call.33
  1030.2 11.7 %cholesky.255 = f32[128,128]{1,0:T(8,128)S(1)} custom-call(f32[128,128]{1,0:T(8,128)S(1)} %convolution_subtract_fusion.5), custom_call_target="Cholesky" | custom-call | tf_op jit(solution)/shard_map/jit(cholesky)/cholesky | solution.py:116
  1047.8 14.1 %while.1 = (s32[]{:T(128)}, f32[512,512]{1,0:T(8,128)}, s32[4,2]{0,1:T(2,128)S(1)}, f32[4,128,128]{2,1,0:T(8,128)}, s32[]{:T(128)}) while((s32[]{:T(128)}, f32[512,512]{1,0:T(8,128)}, s32[4,2]{0,1:T(2,128)S(1)}, f32[4,128,128]{2,1,0:T(8,128)}, s32[]{:T(128)}) %tuple.46), condition=%wide.while_cond, body=%wide.while_body.sunk | while | flops 2 | bytes 132205 | solution.py:118
  1061.9 40.1 %custom-call.34 = f32[4,128,128]{1,2,0:T(8,128)S(1)} custom-call(f32[4,128,128]{2,1,0:T(8,128)} %get-tuple-element.12), custom_call_target="InvertDiagBlocksLowerTriangular" | custom-call | tf_op jit(solution)/shard_map/jit(_solve_triangular)/triangular_solve | solution.py:118
  1108.7 4.8 fusion.30
  (210 shorter events, 180.7 us)
Async XLA Ops:
  8.1 6.2 copy-start.21
  8.1 8.3 copy-start.20
  8.1 23.5 %copy-start.1 = (f32[2,16,128,128]{3,2,1,0:T(8,128)S(1)}, f32[2,16,128,128]{3,2,1,0:T(8,128)}, u32[]{:S(2)}) copy-start(f32[2,16,128,128]{3,2,1,0:T(8,128)} %param.6) | copy-start | bytes 6291460
  18.6 43.7 %all-to-all-start = ((f32[64,1,1]{2,1,0:T(1,128)}), f32[64,1,1]{2,1,0:T(1,128)S(1)}, u32[]{:S(2)}, u32[]{:S(2)}) async-start(f32[64,1,1]{2,1,0:T(1,128)} %broadcast_in_dim.49), calls=%async_computation | async-start | bytes 65536 | tf_op jit(solution)/shard_map/all_to_all | solution.py:25
  33.1 57.2 %collective-permute-start.1 = (f32[1,16,128,128]{3,2,1,0:T(8,128)}, f32[1,16,128,128]{3,2,1,0:T(8,128)}, u32[]{:S(2)}, u32[]{:S(2)}) collective-permute-start(f32[1,16,128,128]{3,2,1,0:T(8,128)} %get-tuple-element.37), channel_id=1, source_target_pairs={{4,0},{8,4},{12,8},{16,12},{20,16},{24,20},{28,24},{32,28},{36,32}... | collective-permute-start | bytes 3145736 | tf_op jit(solution)/shard_map/ppermute | solution.py:18
  35.8 54.5 %collective-permute-start = (f32[1,16,128,128]{3,2,1,0:T(8,128)}, f32[1,16,128,128]{3,2,1,0:T(8,128)}, u32[]{:S(2)}, u32[]{:S(2)}) collective-permute-start(f32[1,16,128,128]{3,2,1,0:T(8,128)} %get-tuple-element.38), channel_id=1, source_target_pairs={{0,4},{4,8},{8,12},{12,16},{16,20},{20,24},{24,28},{28,32},{32,36}... | collective-permute-start | bytes 3145736 | tf_op jit(solution)/shard_map/ppermute | solution.py:17
  45.8 3.3 copy-start.6
  49.1 2.3 copy-start.7
  63.5 21.4 %all-to-all-start.1 = ((f32[64,1,1]{2,1,0:T(1,128)}), f32[64,1,1]{2,1,0:T(1,128)S(1)}, u32[]{:S(2)}, u32[]{:S(2)}) async-start(f32[64,1,1]{2,1,0:T(1,128)} %broadcast_in_dim.50), calls=%async_computation.1 | async-start | bytes 65536 | tf_op jit(solution)/shard_map/all_to_all | solution.py:25
  75.5 275.6 %all-reduce.4.cloned.1.call-start = ((), (), s32[]{:S(2)}) async-start(), calls=%async_computation.3 | async-start | bytes 2097152 | tf_op jit(solution)/shard_map/psum | solution.py:115
  131.9 26.2 %collective-permute-start.3 = (f32[1,16,128,128]{3,2,1,0:T(8,128)}, f32[1,16,128,128]{3,2,1,0:T(8,128)}, u32[]{:S(2)}, u32[]{:S(2)}) collective-permute-start(f32[1,16,128,128]{3,2,1,0:T(8,128)} %get-tuple-element.33), channel_id=1, source_target_pairs={{4,0},{8,4},{12,8},{16,12},{20,16},{24,20},{28,24},{32,28},{36,32}... | collective-permute-start | bytes 3145736 | tf_op jit(solution)/shard_map/ppermute | solution.py:18
  133.5 24.7 %collective-permute-start.2 = (f32[1,16,128,128]{3,2,1,0:T(8,128)S(1)}, f32[1,16,128,128]{3,2,1,0:T(8,128)}, u32[]{:S(2)}, u32[]{:S(2)}) collective-permute-start(f32[1,16,128,128]{3,2,1,0:T(8,128)S(1)} %get-tuple-element.34), channel_id=1, source_target_pairs={{0,4},{4,8},{8,12},{12,16},{16,20},{20,24},{24,28},{28,32},{32,36}... | collective-permute-start | bytes 3145736 | tf_op jit(solution)/shard_map/ppermute | solution.py:17
  148.6 3.3 copy-start.14
  170.1 3.3 copy-start.16
  196.6 7.2 copy-start.23
  196.6 7.2 copy-start.4
  199.8 23.4 %collective-permute-start.5 = (f32[1,16,128,128]{3,2,1,0:T(8,128)}, f32[1,16,128,128]{3,2,1,0:T(8,128)}, u32[]{:S(2)}, u32[]{:S(2)}) collective-permute-start(f32[1,16,128,128]{3,2,1,0:T(8,128)} %get-tuple-element.29), channel_id=1, source_target_pairs={{4,0},{8,4},{12,8},{16,12},{20,16},{24,20},{28,24},{32,28},{36,32}... | collective-permute-start | bytes 3145736 | tf_op jit(solution)/shard_map/ppermute | solution.py:18
  203.6 24.1 %collective-permute-start.4 = (f32[1,16,128,128]{3,2,1,0:T(8,128)}, f32[1,16,128,128]{3,2,1,0:T(8,128)}, u32[]{:S(2)}, u32[]{:S(2)}) collective-permute-start(f32[1,16,128,128]{3,2,1,0:T(8,128)} %get-tuple-element.30), channel_id=1, source_target_pairs={{0,4},{4,8},{8,12},{12,16},{16,20},{20,24},{24,28},{28,32},{32,36}... | collective-permute-start | bytes 3145736 | tf_op jit(solution)/shard_map/ppermute | solution.py:17
  211.9 3.3 copy-start.12
  238.9 3.3 copy-start.15
  300.0 4.5 copy-start.5
  304.6 650.0 %all-reduce.6.cloned.1.call-start = ((), (), s32[]{:S(2)}) async-start(), calls=%async_computation.4 | async-start | bytes 2097152 | tf_op jit(solution)/shard_map/psum | solution.py:115
  954.6 2.6 copy-start.17
  1047.8 57.2 %copy-start.18 = (f32[512,512]{1,0:T(8,128)S(1)}, f32[512,512]{1,0:T(8,128)}, u32[]{:S(2)}) copy-start(f32[512,512]{1,0:T(8,128)} %fusion.46) | copy-start | bytes 3145732
  (10 other events, 20.7 us)
Sparse Core Ops, SparseCore 0:
  304.7 46.4 all-reduce.3
  353.8 600.8 all-reduce.5
